TPU v7x, 256 devices: a whole 4x4x8 slice. The times are simulated.
256 devices in a mesh: dp: 2 (over core), seq: 8 (over z), expert: 16 (over y, x).
Axes of the slice: x: 4, y: 4, z: 8, core: 2. Of those that a mesh axis runs over, the one named last changes fastest.
Arguments:
- tokens: bfloat16 [16384, 2048], P(('dp', 'seq')), may hold values from -6 to 6
- phi: bfloat16 [2048, 32], P(None, 'expert'), may hold values from -40 to 40
- w_in: bfloat16 [32, 2048, 8192], P('expert', None, ('dp', 'seq')), may hold values from -1 to 1
- w_out: bfloat16 [32, 8192, 2048], P('expert', ('dp', 'seq')), may hold values from -0.25 to 0.25
Outputs:
- mixed: bfloat16 [16384, 2048], P(('dp', 'seq', 'expert'))
All inputs are finite; a program needn't handle non-finite values.
Results may differ from a plain program's by a relative error of at most 0.0068.
Values may be sent and summed in bfloat16 or wider, within the bound.
A program may use at most 64 MiB of HBM per device.

v0:
```python
import jax
import jax.numpy as jnp
from jax import lax
from jax.sharding import PartitionSpec as P


def on_device(tokens, phi, w_in, w_out):
    n_expert = lax.axis_size("expert")
    rows_out = tokens.shape[0] // n_expert
    phi_all = lax.all_gather(phi, "expert", axis=1, tiled=True)
    logits = lax.dot_general(
        phi, tokens, (((0,), (1,)), ((), ())), preferred_element_type=jnp.float32
    )
    slot_max = lax.pmax(jnp.max(logits, axis=1), "seq")
    spread = jnp.exp(logits - slot_max[:, None])
    numerator = jnp.dot(spread.astype(jnp.bfloat16), tokens, preferred_element_type=jnp.float32)
    denominator = jnp.sum(spread, axis=1)
    numer_seq, denom_seq = lax.psum((numerator, denominator), "seq")
    own_slots = (numer_seq / denom_seq[:, None]).astype(jnp.bfloat16)
    slot_in = lax.all_gather(own_slots[None], "dp", axis=0, tiled=True)
    hidden = jax.nn.gelu(
        jnp.einsum("ced,edf->cef", slot_in, w_in, preferred_element_type=jnp.float32),
        approximate=True,
    ).astype(jnp.bfloat16)
    partial_value = jnp.einsum("cef,efd->ced", hidden, w_out, preferred_element_type=jnp.float32)
    totals = lax.psum(partial_value, ("dp", "seq"))
    summed = lax.dynamic_index_in_dim(totals, lax.axis_index("dp"), 0, keepdims=False)
    slot_out = lax.all_gather(summed.astype(jnp.bfloat16), "expert", axis=0, tiled=True)
    rows = lax.dynamic_slice_in_dim(tokens, lax.axis_index("expert") * rows_out, rows_out, 0)
    row_logits = lax.dot_general(
        phi_all, rows, (((0,), (1,)), ((), ())), preferred_element_type=jnp.float32
    )
    row_max = jnp.max(row_logits, axis=0)
    combine_weights = jnp.exp(row_logits - row_max[None, :])
    mixed_numer = lax.dot_general(
        combine_weights.astype(jnp.bfloat16),
        slot_out,
        (((0,), (0,)), ((), ())),
        preferred_element_type=jnp.float32,
    )
    mixed_denom = jnp.sum(combine_weights, axis=0)
    return (mixed_numer / mixed_denom[:, None]).astype(jnp.bfloat16)


def solution(mesh):
    placed = (
        P(("dp", "seq"), None),
        P(None, "expert"),
        P("expert", None, ("dp", "seq")),
        P("expert", ("dp", "seq"), None),
    )
    return jax.shard_map(
        on_device,
        mesh=mesh,
        in_specs=placed,
        out_specs=P(("dp", "seq", "expert"), None),
        check_vma=False,
    )
```

profile of v0, /device:TPU:32, one launch (start us, length us, event | category | flops | bytes accessed | tf_op | source)
XLA Modules:
  0.0 159.4 jit_solution(6288700102996713554)
XLA Ops:
  0.0 3.5 %fusion.39 = (f32[2]{0:T(128)S(1)}, f32[2,1024]{1,0:T(2,128)S(1)}) fusion(bf16[2048,2]{0,1:T(2,128)(2,1)} %param.5, bf16[1024,2048]{1,0:T(8,128)(2,1)} %param.4), kind=kOutput, calls=%fused_computation.39 | convolution fusion | flops 8390654 | bytes 4210696 | tf_op jit(solution)/shard_map/dot_general | solution.py:11
  3.5 17.9 %pmax.7 = f32[2]{0:T(128)S(1)} all-reduce(f32[2]{0:T(128)S(1)} %get-tuple-element.9), channel_id=1, replica_groups=mesh['dp'=2,'seq'=8,'expert'=16] {'seq'}, use_global_device_ids=true, to_apply=%region_2.0 | all-reduce | flops 2 | bytes 16 | tf_op jit(solution)/shard_map/pmax | solution.py:14
  21.4 0.2 fusion.25
  21.6 2.9 %fusion.27 = f32[2,2048]{1,0:T(2,128)S(1)} fusion(bf16[1024,2048]{1,0:T(8,128)(2,1)} %param.4, f32[2,1024]{1,0:T(2,128)S(1)} %get-tuple-element.10, f32[2]{0:T(128)S(1)} %pmax.7), kind=kOutput, calls=%fused_computation.28 | convolution fusion | flops 8392704 | bytes 4218888 | tf_op jit(solution)/shard_map/dot_general | solution.py:16
  24.5 27.9 %all-reduce = (f32[2,2048]{1,0:T(2,128)S(1)}, f32[2]{0:T(128)S(1)}) all-reduce(f32[2,2048]{1,0:T(2,128)S(1)} %fusion.27, f32[2]{0:T(128)S(1)} %fusion.25), channel_id=1, replica_groups=mesh['dp'=2,'seq'=8,'expert'=16] {'seq'}, use_global_device_ids=true, to_apply=%region_3.0 | all-reduce | flops 4098 | bytes 32784 | tf_op jit(solution)/shard_map/psum | solution.py:18
  52.4 0.1 fusion.24
  52.5 1.8 %all-gather.3 = bf16[2,2,2048]{2,1,0:T(2,128)(2,1)S(1)} all-gather(bf16[1,2,2048]{2,1,0:T(2,128)(2,1)S(1)} %fusion.24), channel_id=2, replica_groups=mesh['dp'=2,'seq'=8,'expert'=16] {'dp'}, dimensions={0}, use_global_device_ids=true | all-gather | bytes 24576 | tf_op jit(solution)/shard_map/all_gather | solution.py:20
  54.3 0.0 copy-start
  54.3 4.7 %convolution_bitcast_fusion = f32[2,2,2048]{2,0,1:T(2,128)S(1)} fusion(bf16[2,512,2048]{2,1,0:T(8,128)(2,1)} %param.7, bf16[2,2048,512]{2,1,0:T(8,128)(2,1)} %param.6, bf16[2,2,2048]{2,1,0:T(2,128)(2,1)S(1)} %all-gather.3), kind=kOutput, calls=%fused_computation.2 | convolution fusion | flops 16795648 | bytes 8437760 | tf_op jit(solution)/shard_map/cef,efd->ced/dot_general | solution.py:25
  59.0 51.1 %psum.23 = bf16[2,2,2048]{2,0,1:T(2,128)(2,1)S(1)} all-reduce(f32[2,2,2048]{2,0,1:T(2,128)S(1)} %convolution_bitcast_fusion), channel_id=1, replica_groups=mesh['dp'=2,'seq'=8,'expert'=16] {'dp','seq'}, use_global_device_ids=true, to_apply=%region_6.7 | all-reduce | flops 8192 | bytes 49152 | tf_op jit(solution)/shard_map/psum | solution.py:26
  110.1 0.0 copy-done
  110.1 24.0 %all-gather.2 = bf16[16,2,2048]{2,1,0:T(2,128)(2,1)S(1)} all-gather(bf16[1,2,2048]{2,1,0:T(2,128)(2,1)S(1)} %bitcast.24), channel_id=1, replica_groups=mesh['dp'=2,'seq'=8,'expert'=16] {'expert'}, dimensions={0}, use_global_device_ids=true | all-gather | bytes 139264 | tf_op jit(solution)/shard_map/all_gather | solution.py:10
  134.1 0.1 reshape.8
  134.1 1.2 fusion.38
  135.3 23.1 %all-gather.1 = bf16[1,32,2048]{2,0,1:T(2,128)(2,1)S(1)} all-gather(bf16[1,2,2048]{2,0,1:T(2,128)(2,1)S(1)} %dynamic-slice_convert_fusion), channel_id=3, replica_groups=mesh['dp'=2,'seq'=8,'expert'=16] {'expert'}, dimensions={1}, use_global_device_ids=true | all-gather | bytes 139264 | tf_op jit(solution)/shard_map/all_gather | solution.py:28
  158.4 1.0 fusion
  (2 shorter events, 0.1 us)
Async XLA Ops:
  54.3 55.8 %copy-start = (bf16[2048,2]{0,1:T(2,128)(2,1)S(1)}, bf16[2048,2]{0,1:T(2,128)(2,1)}, u32[]{:S(2)}) copy-start(bf16[2048,2]{0,1:T(2,128)(2,1)} %param.5) | copy-start | bytes 24580
where the time goes:
time: 160 us; the launch traced here: 159 us
  blocking collectives  146 us (91%)
  matrix products  13.2 us (8%)
    psum x1, blocking collectives, on_device(): totals = lax.psum(partial_value, ('dp', 'seq'))  51.1 us
    psum x1, blocking collectives, on_device(): numer_seq, denom_seq = lax.psum((numerator, denominator), 'seq')  27.9 us
    all_gather x1, blocking collectives, on_device(): phi_all = lax.all_gather(phi, 'expert', axis=1, tiled=True)  24 us
    all_gather x1, blocking collectives, on_device(): lax.all_gather(summed.astype(jnp.bfloat16), 'expert', axis=0, tiled=True)  23.1 us
    pmax x1, blocking collectives, on_device(): slot_max = lax.pmax(jnp.max(logits, axis=1), 'seq')  17.9 us
    dot_general x1, matrix products, on_device(): jnp.einsum('cef,efd->ced', hidden, w_out, preferred_element_type=jnp.floa...  4.66 us
    dot_general x1, matrix products, on_device(): lax.dot_general(phi, tokens, (((0,), (1,)), ((), ())), preferred_element_...  3.5 us

commit v1 on v0

--- a/solution.py
+++ b/solution.py
@@ -4,10 +4,28 @@
 from jax.sharding import PartitionSpec as P
 
 
+def ring_gather(array, axis, dim):
+    ways, here, hop = (lax.axis_size(axis), lax.axis_index(axis), array.shape[dim])
+    dims = [n * ways if d == dim else n for d, n in enumerate(array.shape)]
+    full = lax.dynamic_update_slice_in_dim(
+        jnp.zeros(dims, array.dtype), array, here * hop, axis=dim
+    )
+    going_up = going_down = array
+    for far in range(1, ways // 2 + 1):
+        going_up = lax.ppermute(going_up, axis, [(d, (d + 1) % ways) for d in range(ways)])
+        full = lax.dynamic_update_slice_in_dim(full, going_up, (here - far) % ways * hop, axis=dim)
+        if 2 * far < ways:
+            going_down = lax.ppermute(going_down, axis, [(d, (d - 1) % ways) for d in range(ways)])
+            full = lax.dynamic_update_slice_in_dim(
+                full, going_down, (here + far) % ways * hop, axis=dim
+            )
+    return full
+
+
 def on_device(tokens, phi, w_in, w_out):
     n_expert = lax.axis_size("expert")
     rows_out = tokens.shape[0] // n_expert
-    phi_all = lax.all_gather(phi, "expert", axis=1, tiled=True)
+    phi_all = ring_gather(phi, "expert", 1)
     logits = lax.dot_general(
         phi, tokens, (((0,), (1,)), ((), ())), preferred_element_type=jnp.float32
     )

time: 160 us -> 190 us (1.19)
  starting transfers between devices: 0 us -> 37.5 us
  blocking collectives: 146 us -> 121 us
  waiting for transfers between devices: 0 us -> 16.4 us
    ppermute x0 -> x15, starting transfers between devices: none -> 37.5 us  [the longest x7 35.8 us: ring_gather(): lax.ppermute(going_down, axis, [(d, (d - 1) % ways) for d in range(ways)])]
    all_gather x1 -> x0, blocking collectives: 24 us -> none  [on_device(): phi_all = lax.all_gather(phi, 'expert', axis=1, tiled=True)]
    ppermute x0 -> x15, waiting for transfers between devices: none -> 16.4 us  [the longest x8 16.4 us: ring_gather(): lax.ppermute(going_up, axis, [(d, (d + 1) % ways) for d in range(ways)])]
  transfers between devices with their start and end apart: 0 -> 15, of which waited for: 0 -> 7; matrix products, arithmetic and copies ran while one was open for 0% -> 6% of each run, Pallas kernels for 0% -> 0%
where the time goes in v1:
time: 190 us; the launch traced here: 189 us
  blocking collectives  121 us (64%)
  starting transfers between devices  37.5 us (20%)
  waiting for transfers between devices  16.4 us (9%)
  matrix products  13.2 us (7%)
    psum x1, blocking collectives, on_device(): totals = lax.psum(partial_value, ('dp', 'seq'))  51.1 us
    ppermute x7, starting transfers between devices, ring_gather(): lax.ppermute(going_down, axis, [(d, (d - 1) % ways) for d in range(ways)])  35.8 us
    psum x1, blocking collectives, on_device(): numer_seq, denom_seq = lax.psum((numerator, denominator), 'seq')  27.9 us
    all_gather x1, blocking collectives, on_device(): lax.all_gather(summed.astype(jnp.bfloat16), 'expert', axis=0, tiled=True)  22.6 us
    pmax x1, blocking collectives, on_device(): slot_max = lax.pmax(jnp.max(logits, axis=1), 'seq')  17.9 us
    ppermute x8, waiting for transfers between devices, ring_gather(): lax.ppermute(going_up, axis, [(d, (d + 1) % ways) for d in range(ways)])  16.4 us
    dot_general x1, matrix products, on_device(): jnp.einsum('cef,efd->ced', hidden, w_out, preferred_element_type=jnp.floa...  4.66 us
  transfers between devices with their start and end apart: 15, of which 7 were waited for; matrix products, arithmetic and copies ran while one was open for 6% of the time, Pallas kernels for 0%

profile of v1, /device:TPU:32, one launch (start us, length us, event | category | flops | bytes accessed | tf_op | source)
XLA Modules:
  0.0 189.3 jit_solution(12360647325249847426)
XLA Ops:
  0.0 1.5 collective-permute-start
  1.5 3.9 %collective-permute-start.1 = (bf16[2048,2]{0,1:T(2,128)(2,1)}, bf16[2048,2]{0,1:T(2,128)(2,1)S(1)}, u32[]{:S(2)}, u32[]{:S(2)}) collective-permute-start(bf16[2048,2]{0,1:T(2,128)(2,1)} %param.5), channel_id=1, source_target_pairs={{0,15},{1,0},{2,1},{3,2},{4,3},{5,4},{6,5},{7,6},{8,7},{9,8},{10,9... | collective-permute-start | bytes 24584 | tf_op jit(solution)/shard_map/ppermute | solution.py:18
  5.3 3.5 %fusion.39 = (f32[2]{0:T(128)S(1)}, f32[2,1024]{1,0:T(2,128)S(1)}) fusion(bf16[2048,2]{0,1:T(2,128)(2,1)} %param.5, bf16[1024,2048]{1,0:T(8,128)(2,1)} %param.4), kind=kOutput, calls=%fused_computation.55 | convolution fusion | flops 8390654 | bytes 4210696 | tf_op jit(solution)/shard_map/dot_general | solution.py:29
  8.9 17.9 %pmax.7 = f32[2]{0:T(128)S(1)} all-reduce(f32[2]{0:T(128)S(1)} %get-tuple-element.9), channel_id=1, replica_groups=mesh['dp'=2,'seq'=8,'expert'=16] {'seq'}, use_global_device_ids=true, to_apply=%region_2.3 | all-reduce | flops 2 | bytes 16 | tf_op jit(solution)/shard_map/pmax | solution.py:32
  26.7 0.2 fusion.26
  26.9 2.9 %fusion.28 = f32[2,2048]{1,0:T(2,128)S(1)} fusion(bf16[1024,2048]{1,0:T(8,128)(2,1)} %param.4, f32[2,1024]{1,0:T(2,128)S(1)} %get-tuple-element.10, f32[2]{0:T(128)S(1)} %pmax.7), kind=kOutput, calls=%fused_computation.45 | convolution fusion | flops 8392704 | bytes 4218888 | tf_op jit(solution)/shard_map/dot_general | solution.py:34
  29.8 27.9 %all-reduce = (f32[2,2048]{1,0:T(2,128)S(1)}, f32[2]{0:T(128)S(1)}) all-reduce(f32[2,2048]{1,0:T(2,128)S(1)} %fusion.28, f32[2]{0:T(128)S(1)} %fusion.26), channel_id=1, replica_groups=mesh['dp'=2,'seq'=8,'expert'=16] {'seq'}, use_global_device_ids=true, to_apply=%region_3.4 | all-reduce | flops 4098 | bytes 32784 | tf_op jit(solution)/shard_map/psum | solution.py:36
  57.7 0.1 fusion.24
  57.8 1.8 all-gather.2
  59.6 4.7 %convolution_bitcast_fusion = f32[2,2,2048]{2,0,1:T(2,128)S(1)} fusion(bf16[2,512,2048]{2,1,0:T(8,128)(2,1)} %param.7, bf16[2,2048,512]{2,1,0:T(8,128)(2,1)} %param.6, bf16[2,2,2048]{2,1,0:T(2,128)(2,1)S(1)} %all-gather.2), kind=kOutput, calls=%fused_computation.2 | convolution fusion | flops 16795648 | bytes 8437760 | tf_op jit(solution)/shard_map/cef,efd->ced/dot_general | solution.py:43
  64.3 51.1 %psum.23 = bf16[2,2,2048]{2,0,1:T(2,128)(2,1)S(1)} all-reduce(f32[2,2,2048]{2,0,1:T(2,128)S(1)} %convolution_bitcast_fusion), channel_id=1, replica_groups=mesh['dp'=2,'seq'=8,'expert'=16] {'dp','seq'}, use_global_device_ids=true, to_apply=%region_6.7 | all-reduce | flops 8192 | bytes 49152 | tf_op jit(solution)/shard_map/psum | solution.py:44
  115.4 22.6 %all-gather.1 = bf16[1,32,2048]{2,0,1:T(2,128)(2,1)S(1)} all-gather(bf16[1,2,2048]{2,0,1:T(2,128)(2,1)S(1)} %dynamic-slice_convert_fusion), channel_id=3, replica_groups=mesh['dp'=2,'seq'=8,'expert'=16] {'expert'}, dimensions={1}, use_global_device_ids=true | all-gather | bytes 139264 | tf_op jit(solution)/shard_map/all_gather | solution.py:46
  138.2 0.0 collective-permute-done
  138.2 0.2 collective-permute-start.2
  138.5 5.2 %collective-permute-start.3 = (bf16[2048,2]{0,1:T(2,128)(2,1)S(1)}, bf16[2048,2]{0,1:T(2,128)(2,1)S(1)}, u32[]{:S(2)}, u32[]{:S(2)}) collective-permute-start(bf16[2048,2]{0,1:T(2,128)(2,1)S(1)} %collective-permute-done.1), channel_id=1, source_target_pairs={{0,15},{1,0},{2,1},{3,2},{4,3},{5,4},{6,5},{7,6},{8,7},{9,8},{10,9... | collective-permute-start | bytes 24584 | tf_op jit(solution)/shard_map/ppermute | solution.py:18
  143.7 1.6 collective-permute-done.2
  145.3 0.0 collective-permute-start.4
  145.3 0.0 collective-permute-done.3
  145.3 5.3 %collective-permute-start.5 = (bf16[2048,2]{0,1:T(2,128)(2,1)S(1)}, bf16[2048,2]{0,1:T(2,128)(2,1)S(1)}, u32[]{:S(2)}, u32[]{:S(2)}) collective-permute-start(bf16[2048,2]{0,1:T(2,128)(2,1)S(1)} %collective-permute-done.3), channel_id=1, source_target_pairs={{0,15},{1,0},{2,1},{3,2},{4,3},{5,4},{6,5},{7,6},{8,7},{9,8},{10,9... | collective-permute-start | bytes 24584 | tf_op jit(solution)/shard_map/ppermute | solution.py:18
  150.7 1.6 collective-permute-done.4
  152.3 5.3 %collective-permute-start.7 = (bf16[2048,2]{0,1:T(2,128)(2,1)S(1)}, bf16[2048,2]{0,1:T(2,128)(2,1)S(1)}, u32[]{:S(2)}, u32[]{:S(2)}) collective-permute-start(bf16[2048,2]{0,1:T(2,128)(2,1)S(1)} %collective-permute-done.5), channel_id=1, source_target_pairs={{0,15},{1,0},{2,1},{3,2},{4,3},{5,4},{6,5},{7,6},{8,7},{9,8},{10,9... | collective-permute-start | bytes 24584 | tf_op jit(solution)/shard_map/ppermute | solution.py:18
  157.7 1.6 collective-permute-done.6
  159.2 5.3 %collective-permute-start.9 = (bf16[2048,2]{0,1:T(2,128)(2,1)S(1)}, bf16[2048,2]{0,1:T(2,128)(2,1)S(1)}, u32[]{:S(2)}, u32[]{:S(2)}) collective-permute-start(bf16[2048,2]{0,1:T(2,128)(2,1)S(1)} %collective-permute-done.7), channel_id=1, source_target_pairs={{0,15},{1,0},{2,1},{3,2},{4,3},{5,4},{6,5},{7,6},{8,7},{9,8},{10,9... | collective-permute-start | bytes 24584 | tf_op jit(solution)/shard_map/ppermute | solution.py:18
  164.6 1.6 collective-permute-done.8
  166.2 0.0 collective-permute-start.10
  166.2 5.3 %collective-permute-start.11 = (bf16[2048,2]{0,1:T(2,128)(2,1)S(1)}, bf16[2048,2]{0,1:T(2,128)(2,1)S(1)}, u32[]{:S(2)}, u32[]{:S(2)}) collective-permute-start(bf16[2048,2]{0,1:T(2,128)(2,1)S(1)} %collective-permute-done.9), channel_id=1, source_target_pairs={{0,15},{1,0},{2,1},{3,2},{4,3},{5,4},{6,5},{7,6},{8,7},{9,8},{10,9... | collective-permute-start | bytes 24584 | tf_op jit(solution)/shard_map/ppermute | solution.py:18
  171.6 1.6 collective-permute-done.10
  173.2 5.3 %collective-permute-start.13 = (bf16[2048,2]{0,1:T(2,128)(2,1)S(1)}, bf16[2048,2]{0,1:T(2,128)(2,1)S(1)}, u32[]{:S(2)}, u32[]{:S(2)}) collective-permute-start(bf16[2048,2]{0,1:T(2,128)(2,1)S(1)} %collective-permute-done.11), channel_id=1, source_target_pairs={{0,15},{1,0},{2,1},{3,2},{4,3},{5,4},{6,5},{7,6},{8,7},{9,8},{10,9... | collective-permute-start | bytes 24584 | tf_op jit(solution)/shard_map/ppermute | solution.py:18
  178.6 1.6 collective-permute-done.12
  180.2 6.9 %collective-permute-done.14 = bf16[2048,2]{0,1:T(2,128)(2,1)S(1)} collective-permute-done((bf16[2048,2]{0,1:T(2,128)(2,1)S(1)}, bf16[2048,2]{0,1:T(2,128)(2,1)S(1)}, u32[]{:S(2)}, u32[]{:S(2)}) %collective-permute-start.14) | collective-permute-done | bytes 8224 | tf_op jit(solution)/shard_map/ppermute | solution.py:15
  187.1 1.2 fusion.38
  188.3 1.0 fusion
  (31 shorter events, 0.4 us)
Async XLA Ops:
  0.0 138.2 %collective-permute-start = (bf16[2048,2]{0,1:T(2,128)(2,1)}, bf16[2048,2]{0,1:T(2,128)(2,1)S(1)}, u32[]{:S(2)}, u32[]{:S(2)}) collective-permute-start(bf16[2048,2]{0,1:T(2,128)(2,1)} %param.5), channel_id=1, source_target_pairs={{0,1},{1,2},{2,3},{3,4},{4,5},{5,6},{6,7},{7,8},{8,9},{9,10},{10,1... | collective-permute-start | bytes 24584 | tf_op jit(solution)/shard_map/ppermute | solution.py:15
  1.5 137.0 %collective-permute-start.1 = (bf16[2048,2]{0,1:T(2,128)(2,1)}, bf16[2048,2]{0,1:T(2,128)(2,1)S(1)}, u32[]{:S(2)}, u32[]{:S(2)}) collective-permute-start(bf16[2048,2]{0,1:T(2,128)(2,1)} %param.5), channel_id=1, source_target_pairs={{0,15},{1,0},{2,1},{3,2},{4,3},{5,4},{6,5},{7,6},{8,7},{9,8},{10,9... | collective-permute-start | bytes 24584 | tf_op jit(solution)/shard_map/ppermute | solution.py:18
  59.6 78.4 %copy-start = (bf16[2048,2]{0,1:T(2,128)(2,1)S(1)}, bf16[2048,2]{0,1:T(2,128)(2,1)}, u32[]{:S(2)}) copy-start(bf16[2048,2]{0,1:T(2,128)(2,1)} %param.5) | copy-start | bytes 24580
  138.2 7.0 %collective-permute-start.2 = (bf16[2048,2]{0,1:T(2,128)(2,1)S(1)}, bf16[2048,2]{0,1:T(2,128)(2,1)S(1)}, u32[]{:S(2)}, u32[]{:S(2)}) collective-permute-start(bf16[2048,2]{0,1:T(2,128)(2,1)S(1)} %collective-permute-done), channel_id=1, source_target_pairs={{0,1},{1,2},{2,3},{3,4},{4,5},{5,6},{6,7},{7,8},{8,9},{9,10},{10,1... | collective-permute-start | bytes 24584 | tf_op jit(solution)/shard_map/ppermute | solution.py:15
  138.5 6.8 %collective-permute-start.3 = (bf16[2048,2]{0,1:T(2,128)(2,1)S(1)}, bf16[2048,2]{0,1:T(2,128)(2,1)S(1)}, u32[]{:S(2)}, u32[]{:S(2)}) collective-permute-start(bf16[2048,2]{0,1:T(2,128)(2,1)S(1)} %collective-permute-done.1), channel_id=1, source_target_pairs={{0,15},{1,0},{2,1},{3,2},{4,3},{5,4},{6,5},{7,6},{8,7},{9,8},{10,9... | collective-permute-start | bytes 24584 | tf_op jit(solution)/shard_map/ppermute | solution.py:18
  145.3 7.0 %collective-permute-start.4 = (bf16[2048,2]{0,1:T(2,128)(2,1)S(1)}, bf16[2048,2]{0,1:T(2,128)(2,1)S(1)}, u32[]{:S(2)}, u32[]{:S(2)}) collective-permute-start(bf16[2048,2]{0,1:T(2,128)(2,1)S(1)} %collective-permute-done.2), channel_id=1, source_target_pairs={{0,1},{1,2},{2,3},{3,4},{4,5},{5,6},{6,7},{7,8},{8,9},{9,10},{10,1... | collective-permute-start | bytes 24584 | tf_op jit(solution)/shard_map/ppermute | solution.py:15
  145.3 7.0 %collective-permute-start.5 = (bf16[2048,2]{0,1:T(2,128)(2,1)S(1)}, bf16[2048,2]{0,1:T(2,128)(2,1)S(1)}, u32[]{:S(2)}, u32[]{:S(2)}) collective-permute-start(bf16[2048,2]{0,1:T(2,128)(2,1)S(1)} %collective-permute-done.3), channel_id=1, source_target_pairs={{0,15},{1,0},{2,1},{3,2},{4,3},{5,4},{6,5},{7,6},{8,7},{9,8},{10,9... | collective-permute-start | bytes 24584 | tf_op jit(solution)/shard_map/ppermute | solution.py:18
  152.3 7.0 %collective-permute-start.6 = (bf16[2048,2]{0,1:T(2,128)(2,1)S(1)}, bf16[2048,2]{0,1:T(2,128)(2,1)S(1)}, u32[]{:S(2)}, u32[]{:S(2)}) collective-permute-start(bf16[2048,2]{0,1:T(2,128)(2,1)S(1)} %collective-permute-done.4), channel_id=1, source_target_pairs={{0,1},{1,2},{2,3},{3,4},{4,5},{5,6},{6,7},{7,8},{8,9},{9,10},{10,1... | collective-permute-start | bytes 24584 | tf_op jit(solution)/shard_map/ppermute | solution.py:15
  152.3 7.0 %collective-permute-start.7 = (bf16[2048,2]{0,1:T(2,128)(2,1)S(1)}, bf16[2048,2]{0,1:T(2,128)(2,1)S(1)}, u32[]{:S(2)}, u32[]{:S(2)}) collective-permute-start(bf16[2048,2]{0,1:T(2,128)(2,1)S(1)} %collective-permute-done.5), channel_id=1, source_target_pairs={{0,15},{1,0},{2,1},{3,2},{4,3},{5,4},{6,5},{7,6},{8,7},{9,8},{10,9... | collective-permute-start | bytes 24584 | tf_op jit(solution)/shard_map/ppermute | solution.py:18
  159.2 7.0 %collective-permute-start.8 = (bf16[2048,2]{0,1:T(2,128)(2,1)S(1)}, bf16[2048,2]{0,1:T(2,128)(2,1)S(1)}, u32[]{:S(2)}, u32[]{:S(2)}) collective-permute-start(bf16[2048,2]{0,1:T(2,128)(2,1)S(1)} %collective-permute-done.6), channel_id=1, source_target_pairs={{0,1},{1,2},{2,3},{3,4},{4,5},{5,6},{6,7},{7,8},{8,9},{9,10},{10,1... | collective-permute-start | bytes 24584 | tf_op jit(solution)/shard_map/ppermute | solution.py:15
  159.2 7.0 %collective-permute-start.9 = (bf16[2048,2]{0,1:T(2,128)(2,1)S(1)}, bf16[2048,2]{0,1:T(2,128)(2,1)S(1)}, u32[]{:S(2)}, u32[]{:S(2)}) collective-permute-start(bf16[2048,2]{0,1:T(2,128)(2,1)S(1)} %collective-permute-done.7), channel_id=1, source_target_pairs={{0,15},{1,0},{2,1},{3,2},{4,3},{5,4},{6,5},{7,6},{8,7},{9,8},{10,9... | collective-permute-start | bytes 24584 | tf_op jit(solution)/shard_map/ppermute | solution.py:18
  166.2 7.0 %collective-permute-start.10 = (bf16[2048,2]{0,1:T(2,128)(2,1)S(1)}, bf16[2048,2]{0,1:T(2,128)(2,1)S(1)}, u32[]{:S(2)}, u32[]{:S(2)}) collective-permute-start(bf16[2048,2]{0,1:T(2,128)(2,1)S(1)} %collective-permute-done.8), channel_id=1, source_target_pairs={{0,1},{1,2},{2,3},{3,4},{4,5},{5,6},{6,7},{7,8},{8,9},{9,10},{10,1... | collective-permute-start | bytes 24584 | tf_op jit(solution)/shard_map/ppermute | solution.py:15
  166.2 7.0 %collective-permute-start.11 = (bf16[2048,2]{0,1:T(2,128)(2,1)S(1)}, bf16[2048,2]{0,1:T(2,128)(2,1)S(1)}, u32[]{:S(2)}, u32[]{:S(2)}) collective-permute-start(bf16[2048,2]{0,1:T(2,128)(2,1)S(1)} %collective-permute-done.9), channel_id=1, source_target_pairs={{0,15},{1,0},{2,1},{3,2},{4,3},{5,4},{6,5},{7,6},{8,7},{9,8},{10,9... | collective-permute-start | bytes 24584 | tf_op jit(solution)/shard_map/ppermute | solution.py:18
  173.2 7.0 %collective-permute-start.12 = (bf16[2048,2]{0,1:T(2,128)(2,1)S(1)}, bf16[2048,2]{0,1:T(2,128)(2,1)S(1)}, u32[]{:S(2)}, u32[]{:S(2)}) collective-permute-start(bf16[2048,2]{0,1:T(2,128)(2,1)S(1)} %collective-permute-done.10), channel_id=1, source_target_pairs={{0,1},{1,2},{2,3},{3,4},{4,5},{5,6},{6,7},{7,8},{8,9},{9,10},{10,1... | collective-permute-start | bytes 24584 | tf_op jit(solution)/shard_map/ppermute | solution.py:15
  173.2 7.0 %collective-permute-start.13 = (bf16[2048,2]{0,1:T(2,128)(2,1)S(1)}, bf16[2048,2]{0,1:T(2,128)(2,1)S(1)}, u32[]{:S(2)}, u32[]{:S(2)}) collective-permute-start(bf16[2048,2]{0,1:T(2,128)(2,1)S(1)} %collective-permute-done.11), channel_id=1, source_target_pairs={{0,15},{1,0},{2,1},{3,2},{4,3},{5,4},{6,5},{7,6},{8,7},{9,8},{10,9... | collective-permute-start | bytes 24584 | tf_op jit(solution)/shard_map/ppermute | solution.py:18
  180.2 7.0 %collective-permute-start.14 = (bf16[2048,2]{0,1:T(2,128)(2,1)S(1)}, bf16[2048,2]{0,1:T(2,128)(2,1)S(1)}, u32[]{:S(2)}, u32[]{:S(2)}) collective-permute-start(bf16[2048,2]{0,1:T(2,128)(2,1)S(1)} %collective-permute-done.12), channel_id=1, source_target_pairs={{0,1},{1,2},{2,3},{3,4},{4,5},{5,6},{6,7},{7,8},{8,9},{9,10},{10,1... | collective-permute-start | bytes 24584 | tf_op jit(solution)/shard_map/ppermute | solution.py:15
